TPU v7x, 32 devices: a whole 2x2x4 slice. The times are simulated.
32 devices in a mesh: grp: 2 (over y), pair: 4 (over z), aux: 2 (over x), rep: 2 (over core).
Axes of the slice: x: 2, y: 2, z: 4, core: 2. Of those that a mesh axis runs over, the one named last changes fastest.
Arguments:
- three_center: bfloat16 [5120, 4, 8000], P(('grp', 'aux', 'rep', 'pair')), parts along dimension 0, may hold values from -0.050591038 to 0.050591038
- eps_occ: float32 [8], P('grp'), parts along dimension 0, may hold values from -1.2 to -0.4
- eps_virt: float32 [16000], P(('grp', 'pair')), parts along dimension 0, may hold values from 0.2 to 3
- freq: float32 [2], P('grp'), parts along dimension 0, may hold values from 0.2 to 2
Outputs:
- polar: float32 [5120, 2560], P(('grp', 'aux', 'rep'), 'pair'), parts along dimension 0
There are 2 independent parts, one for each index of `grp`. A program takes and returns all parts, laid end to end along the dimension named above; each array names one. Nothing has to cross between parts.
All inputs are finite; a program needn't handle non-finite values.
Results may differ from a plain program's by a relative error of at most 0.0003.
Values may be sent and summed in bfloat16 or wider, within the bound.
A program may use at most 192 MiB of HBM per device.

v0:
```python
import jax
import jax.numpy as jnp
from jax import lax
from jax.sharding import PartitionSpec as P


def local(three_center, eps_occ, eps_virt, freq):
    arrived = lax.all_to_all(three_center, "pair", split_axis=2, concat_axis=0, tiled=True)
    excite = eps_virt[None, :] - eps_occ[:, None]
    weight = 2.0 * excite / (excite * excite + freq[0] * freq[0])
    height = arrived.shape[0]
    scaled = (
        (arrived.astype(jnp.float32) * weight[None, :, :]).astype(jnp.bfloat16).reshape(height, -1)
    )
    plain_rows = arrived.reshape(height, -1)
    partial_sums = lax.dot_general(
        scaled,
        lax.all_gather(plain_rows, ("aux", "rep"), axis=0, tiled=True),
        (((1,), (1,)), ((), ())),
        preferred_element_type=jnp.float32,
    )
    return lax.psum_scatter(partial_sums, "pair", scatter_dimension=1, tiled=True)


def solution(mesh):
    return jax.shard_map(
        local,
        mesh=mesh,
        in_specs=(
            P(("grp", "aux", "rep", "pair"), None, None),
            P("grp"),
            P(("grp", "pair")),
            P("grp"),
        ),
        out_specs=P(("grp", "aux", "rep"), "pair"),
        check_vma=False,
    )
```

profile of v0, /device:TPU:0, one launch (start us, length us, event | category | flops | bytes accessed | tf_op | source)
XLA Modules:
  0.0 865.8 jit_solution(16826013014737475002)
XLA Ops:
  6.5 0.0 copy-start
  6.5 0.0 all-gather.2.cloned.1.call-start
  6.5 32.8 %copy.8 = bf16[160,4,8000]{0,1,2:T(4,128)(2,1)} copy(bf16[160,4,8000]{2,1,0:T(4,128)(2,1)} %param.4) | data formatting | bytes 20480000 | tf_op args[0]
  39.3 367.0 %all_to_all.18 = bf16[160,4,8000]{0,1,2:T(4,128)(2,1)} all-to-all(bf16[160,4,8000]{0,1,2:T(4,128)(2,1)} %copy.8), channel_id=1, replica_groups=mesh['grp'=2,'pair'=4,'aux'=2,'rep'=2] {'pair'}, dimensions={2} | all-to-all | bytes 20480000 | tf_op jit(solution)/shard_map/all_to_all | solution.py:8
  406.3 35.7 %copy.9 = bf16[160,4,4,2000]{3,1,0,2:T(4,128)(2,1)} copy(bf16[160,4,4,2000]{0,1,3,2:T(4,128)(2,1)} %bitcast.4) | data formatting | bytes 20480000 | tf_op jit(solution)/shard_map/all_to_all | solution.py:8
  442.0 0.0 copy-start.2
  442.0 20.3 %all_to_all.16 = bf16[640,8000]{1,0:T(8,128)(2,1)} reshape(bf16[4,160,4,2000]{3,2,1,0:T(4,128)(2,1)} %bitcast.5) | data formatting | bytes 20480000 | tf_op jit(solution)/shard_map/all_to_all | solution.py:8
  462.3 0.0 all-gather.2.cloned.1.call-update
  462.3 0.0 reduce-scatter.2.cloned.1.call-start
  463.0 0.0 copy-done
  463.1 0.1 broadcast_reduce_fusion
  463.2 0.1 sub.24
  463.3 0.0 copy-done.2
  463.3 0.1 sub.22
  463.4 245.1 %all-gather.2.cloned.1.call-done = bf16[2560,8000]{1,0:T(8,128)(2,1)} async-done(((bf16[640,8000]{1,0:T(8,128)(2,1)}), bf16[2560,8000]{1,0:T(8,128)(2,1)}) %all-gather.2.cloned.1.call-update) | async-done | bytes 40960016 | tf_op jit(solution)/shard_map/all_gather | solution.py:18
  708.5 0.0 copy-start.1
  708.5 35.3 %fusion = f32[640,2560]{1,0:T(8,128)} fusion(bf16[2560,8000]{1,0:T(8,128)(2,1)} %all-gather.2.cloned.1.call-done, bf16[640,8000]{1,0:T(8,128)(2,1)} %all_to_all.16, f32[8000]{0:T(1024)S(1)} %add_divide_fusion), kind=kOutput, calls=%fused_computation.1 | convolution fusion | flops 26229760000 | bytes 57785600 | tf_op jit(solution)/shard_map/dot_general | solution.py:16
  743.8 0.0 reduce-scatter.2.cloned.1.call-update
  743.8 115.2 %reduce-scatter.2.cloned.1.call-done = f32[640,640]{1,0:T(8,128)} async-done(((f32[640,2560]{1,0:T(8,128)}), f32[640,640]{1,0:T(8,128)}) %reduce-scatter.2.cloned.1.call-update) | async-done | bytes 1638416 | tf_op jit(solution)/shard_map/reduce_scatter | solution.py:22
  859.0 0.0 copy-done.1
  (2 shorter events, 0.0 us)
Async XLA Ops:
  6.5 456.5 %copy-start = (f32[4]{0:T(128)S(1)}, f32[4]{0:T(128)}, u32[]{:S(2)}) copy-start(f32[4]{0:T(128)} %param.5) | copy-start | bytes 52
  6.5 701.9 %all-gather.2.cloned.1.call-start = ((), (), s32[]{:S(2)}) async-start(), calls=%async_computation.2 | async-start | bytes 51609600 | tf_op jit(solution)/shard_map/all_gather | solution.py:18
  442.0 21.3 %copy-start.2 = (f32[2000]{0:T(1024)S(1)}, f32[2000]{0:T(1024)}, u32[]{:S(2)}) copy-start(f32[2000]{0:T(1024)} %param.6) | copy-start | bytes 24004
  462.3 396.6 %reduce-scatter.2.cloned.1.call-start = ((), (), s32[]{:S(2)}) async-start(), calls=%async_computation.3 | async-start | bytes 8192000 | tf_op jit(solution)/shard_map/reduce_scatter | solution.py:22
  708.5 150.5 %copy-start.1 = (f32[4]{0:T(128)S(1)}, f32[4]{0:T(128)}, u32[]{:S(2)}) copy-start(f32[4]{0:T(128)} %param.5) | copy-start | bytes 52
Sparse Core Ops, SparseCore 0:
  462.5 245.9 all-gather.1
  744.0 115.0 reduce-scatter.1
where the time goes:
time: 869 us; the launch traced here: 866 us
  blocking collectives  367 us (42%)
  waiting for transfers between devices  360 us (41%)
  local copies, waits for them, and re-layouts  89.1 us (10%)
  matrix products  35.3 us (4%)
  between operations  14.1 us (2%)
    all_to_all x1, blocking collectives, local(): lax.all_to_all(three_center, 'pair', split_axis=2, concat_axis=0, tiled=T...  367 us
    all_gather x1, waiting for transfers between devices, local(): lax.all_gather(plain_rows, ('aux', 'rep'), axis=0, tiled=True)  245 us
    reduce_scatter x1, waiting for transfers between devices, local(): lax.psum_scatter(partial_sums, 'pair', scatter_dimension=1, tiled=True)  115 us
    all_to_all x2, local copies, waits for them, and re-layouts, local(): lax.all_to_all(three_center, 'pair', split_axis=2, concat_axis=0, tiled=T...  56 us
    dot_general x1, matrix products, local(): lax.dot_general(scaled, lax.all_gather(plain_rows, ('aux', 'rep'), axis=0...  35.3 us
    unnamed x7, local copies, waits for them, and re-layouts  32.8 us
  transfers between devices with their start and end apart: 2, of which 2 were waited for; matrix products, arithmetic and copies ran while one was open for 0% of the time, Pallas kernels for 0%

commit v1 on v0

--- a/solution.py
+++ b/solution.py
@@ -5,7 +5,11 @@
 
 
 def local(three_center, eps_occ, eps_virt, freq):
-    arrived = lax.all_to_all(three_center, "pair", split_axis=2, concat_axis=0, tiled=True)
+    b_now = lax.axis_size("pair")
+    y = jnp.split(three_center, b_now, 2)
+    last = jnp.stack(y, 0)
+    r_now = lax.all_to_all(last, "pair", 0, 0)
+    arrived = jnp.concatenate(r_now, 0)
     excite = eps_virt[None, :] - eps_occ[:, None]
     weight = 2.0 * excite / (excite * excite + freq[0] * freq[0])
     height = arrived.shape[0]

time: 869 us -> 689 us (0.79)
  blocking collectives: 367 us -> 234 us
  local copies, waits for them, and re-layouts: 89.1 us -> 34.1 us
  other arithmetic: 0.02 us -> 9.79 us
    all_to_all x1, blocking collectives: 367 us -> 234 us  [local(): r_now = lax.all_to_all(last, 'pair', 0, 0)]
    all_to_all x2 -> x0, local copies, waits for them, and re-layouts: 56 us -> none  [local(): lax.all_to_all(three_center, 'pair', split_axis=2, concat_axis=0, tiled=T...]
    unnamed x7 -> x6, local copies, waits for them, and re-layouts: 32.8 us -> 0.01 us
    reshape x0 -> x1, local copies, waits for them, and re-layouts: none -> 20.3 us  [local(): arrived = jnp.concatenate(r_now, 0)]
    another operation x0 -> x1, local copies, waits for them, and re-layouts: none -> 13.5 us  [local(): last = jnp.stack(y, 0)]
    another operation x0 -> x1, other arithmetic: none -> 9.78 us  [local(): last = jnp.stack(y, 0)]
where the time goes in v1:
time: 689 us; the launch traced here: 688 us
  waiting for transfers between devices  361 us (52%)
  blocking collectives  234 us (34%)
  matrix products  35.4 us (5%)
  local copies, waits for them, and re-layouts  34.1 us (5%)
  between operations  14.1 us (2%)
  other arithmetic  9.79 us (1%)
    all_gather x1, waiting for transfers between devices, local(): lax.all_gather(plain_rows, ('aux', 'rep'), axis=0, tiled=True)  245 us
    all_to_all x1, blocking collectives, local(): r_now = lax.all_to_all(last, 'pair', 0, 0)  234 us
    reduce_scatter x1, waiting for transfers between devices, local(): lax.psum_scatter(partial_sums, 'pair', scatter_dimension=1, tiled=True)  115 us
    dot_general x1, matrix products, local(): lax.dot_general(scaled, lax.all_gather(plain_rows, ('aux', 'rep'), axis=0...  35.4 us
    reshape x1, local copies, waits for them, and re-layouts, local(): arrived = jnp.concatenate(r_now, 0)  20.3 us
  transfers between devices with their start and end apart: 2, of which 2 were waited for; matrix products, arithmetic and copies ran while one was open for 0% of the time, Pallas kernels for 0%

profile of v1, /device:TPU:0, one launch (start us, length us, event | category | flops | bytes accessed | tf_op | source)
XLA Modules:
  0.0 688.5 jit_solution(14303969859998400281)
XLA Ops:
  6.5 0.0 copy-start
  6.5 0.0 all-gather.2.cloned.1.call-start
  6.5 13.5 %slice_bitcast_fusion.3 = (bf16[1,160,4,2000]{3,2,1,0:T(4,128)(2,1)S(1)}, bf16[1,160,4,2000]{3,2,1,0:T(4,128)(2,1)S(1)}, bf16[1,160,4,2000]{3,2,1,0:T(4,128)(2,1)S(1)}, bf16[1,160,4,2000]{3,2,1,0:T(4,128)(2,1)S(1)}) fusion(bf16[160,4,8000]{2,1,0:T(4,128)(2,1)} %param.4), kind=kLoop, calls=%fused_computation.7 | loop fusion | bytes 20480000 | tf_op jit(solution)/shard_map/stack | solution.py:10
  20.0 9.8 %pad_maximum_fusion = bf16[4,160,4,2000]{3,2,1,0:T(4,128)(2,1)S(1)} fusion(bf16[1,160,4,2000]{3,2,1,0:T(4,128)(2,1)S(1)} %get-tuple-element.7, bf16[1,160,4,2000]{3,2,1,0:T(4,128)(2,1)S(1)} %get-tuple-element.8, bf16[1,160,4,2000]{3,2,1,0:T(4,128)(2,1)S(1)} %get-tuple-element.6, bf16[1,160,4,2000]{3,2,1,0:T(4,128)(2,1)S(1)} %get-tuple-element.5), kind=kLoop, calls=%fused_computation.1 | loop fusion | flops 15360000 | bytes 20480000 | tf_op jit(solution)/shard_map/stack | solution.py:10
  29.8 234.2 %all_to_all.5 = bf16[4,160,4,2000]{3,2,1,0:T(4,128)(2,1)} all-to-all(bf16[4,160,4,2000]{3,2,1,0:T(4,128)(2,1)S(1)} %pad_maximum_fusion), channel_id=1, replica_groups=mesh['grp'=2,'pair'=4,'aux'=2,'rep'=2] {'pair'}, dimensions={0} | all-to-all | bytes 20480000 | tf_op jit(solution)/shard_map/all_to_all | solution.py:11
  264.0 20.3 %reshape.35 = bf16[640,8000]{1,0:T(8,128)(2,1)} reshape(bf16[4,160,4,2000]{3,2,1,0:T(4,128)(2,1)} %all_to_all.5) | data formatting | bytes 20480000 | tf_op jit(solution)/shard_map/reshape | solution.py:12
  284.3 0.0 copy-start.2
  284.3 0.0 all-gather.2.cloned.1.call-update
  284.4 0.2 reduce-scatter.2.cloned.1.call-start
  285.2 0.0 copy-done
  285.3 0.1 broadcast_reduce_fusion
  285.4 0.1 sub.24
  285.5 0.0 copy-done.2
  285.5 0.1 sub.22
  285.6 245.5 %all-gather.2.cloned.1.call-done = bf16[2560,8000]{1,0:T(8,128)(2,1)} async-done(((bf16[640,8000]{1,0:T(8,128)(2,1)}), bf16[2560,8000]{1,0:T(8,128)(2,1)}) %all-gather.2.cloned.1.call-update) | async-done | bytes 40960016 | tf_op jit(solution)/shard_map/all_gather | solution.py:22
  531.1 0.0 copy-start.1
  531.1 35.4 %fusion = f32[640,2560]{1,0:T(8,128)} fusion(bf16[2560,8000]{1,0:T(8,128)(2,1)} %all-gather.2.cloned.1.call-done, bf16[640,8000]{1,0:T(8,128)(2,1)} %reshape.35, f32[8000]{0:T(1024)S(1)} %add_divide_fusion), kind=kOutput, calls=%fused_computation.2 | convolution fusion | flops 26229760000 | bytes 57785600 | tf_op jit(solution)/shard_map/dot_general | solution.py:20
  566.4 0.0 reduce-scatter.2.cloned.1.call-update
  566.5 115.2 %reduce-scatter.2.cloned.1.call-done = f32[640,640]{1,0:T(8,128)} async-done(((f32[640,2560]{1,0:T(8,128)}), f32[640,640]{1,0:T(8,128)}) %reduce-scatter.2.cloned.1.call-update) | async-done | bytes 1638416 | tf_op jit(solution)/shard_map/reduce_scatter | solution.py:26
  681.6 0.0 copy-done.1
  (2 shorter events, 0.0 us)
Async XLA Ops:
  6.5 278.7 %copy-start = (f32[4]{0:T(128)S(1)}, f32[4]{0:T(128)}, u32[]{:S(2)}) copy-start(f32[4]{0:T(128)} %param.5) | copy-start | bytes 52
  6.5 524.5 %all-gather.2.cloned.1.call-start = ((), (), s32[]{:S(2)}) async-start(), calls=%async_computation.2 | async-start | bytes 51609600 | tf_op jit(solution)/shard_map/all_gather | solution.py:22
  284.3 1.1 copy-start.2
  284.4 397.3 %reduce-scatter.2.cloned.1.call-start = ((), (), s32[]{:S(2)}) async-start(), calls=%async_computation.3 | async-start | bytes 8192000 | tf_op jit(solution)/shard_map/reduce_scatter | solution.py:26
  531.1 150.6 %copy-start.1 = (f32[4]{0:T(128)S(1)}, f32[4]{0:T(128)}, u32[]{:S(2)}) copy-start(f32[4]{0:T(128)} %param.5) | copy-start | bytes 52
Sparse Core Ops, SparseCore 0:
  284.5 246.5 all-gather.1
  566.6 115.0 reduce-scatter.1
